TPU v7x, 32 devices: a whole 2x2x4 slice. The times are simulated.
32 devices in a mesh: bond: 16 (over z, y, x), op: 2 (over core).
Axes of the slice: x: 2, y: 2, z: 4, core: 2. Of those that a mesh axis runs over, the one named last changes fastest.
Arguments:
- wavefunction: float32 [6, 256, 8192], P(None, None, 'bond'), may hold values from -6 to 6
- left_tiles: bfloat16 [16, 16, 2, 128, 128], P('op', None, None, 'bond'), may hold values from -0.375 to 0.375
- right_tiles: bfloat16 [16, 16, 2, 128, 128], P('op', None, None, 'bond'), may hold values from -0.375 to 0.375
- site_operators: float32 [16, 4, 4], P('op'), may hold values from -1.75 to 1.75
- left_charge: int32 [16], replicated, may hold values from 0 to 7, as said below
- right_charge: int32 [16], replicated, may hold values from 0 to 7, as said below
- channel_charge: int32 [16, 2], replicated, may hold values from -1 to 7, as said below
Outputs:
- sigma_one: float32 [6, 256, 8192], P(None, 'bond', 'op')
- sigma_two: float32 [6, 256, 8192], P(None, 'op', 'bond')
Inputs may be any that keep to these rules, and one draw needn't show every extreme that they name: `left_charge`: each charge labels exactly 2 of the left blocks. `right_charge`: each charge labels exactly 2 of the right blocks. `channel_charge`: column 0 is a left charge shift, each of 0 to 7 used by exactly 2 channels; column 1 is a site charge shift, each of -1, 0 and 1 used by 5 or 6 channels.
All inputs are finite; a program needn't handle non-finite values.
Results may differ from a plain program's by a relative error of at most 0.0057.
Values may be sent and summed in bfloat16 or wider, within the bound.
A program may use at most 128 MiB of HBM per device.

v0:
```python
import jax
import jax.numpy as jnp
from jax import lax
from jax.sharding import PartitionSpec as P

M = 2048
B = 128
NQ = 8
DP = 4
NB = 16
NPB = 2


site_charge_table = (0, 1, 1, 2)


def block_sources(charge, offset):
    ordering = jnp.argsort(charge, stable=True)
    target = (charge - offset) % NQ
    slot_index = target[:, None] * NPB + jnp.arange(NPB, dtype=jnp.int32)[None, :]
    return ordering[slot_index]


def site_masks(site_operators, channel_charge):
    site_charge = jnp.array(site_charge_table, dtype=jnp.int32)
    charge_step = site_charge[:, None] - site_charge[None, :]
    allowed = (charge_step[None, :, :] - channel_charge[:, 1][:, None, None]) % NQ == 0
    return jnp.where(allowed, site_operators, jnp.zeros_like(site_operators))


def pick_left(tile_full, left_order, row_class):
    slots = row_class[:, :, None] * NPB + jnp.arange(NPB, dtype=jnp.int32)[None, None, :]
    chosen = left_order[slots]

    def choose_tiles(channel_tiles, channel_rows):
        return channel_tiles[channel_rows]

    return jax.vmap(choose_tiles)(tile_full, chosen)


def right_terms(tile_piece, picked, site_matrix):
    inner_sum = jnp.einsum(
        "cjnab,ckrpjnb->ckrpja", tile_piece, picked, preferred_element_type=jnp.float32
    )
    return jnp.einsum("cpq,ckrqja->ckrpja", site_matrix, inner_sum, precision=lax.Precision.HIGHEST)


def local(
    wavefunction, left_tiles, right_tiles, site_operators, left_charge, right_charge, channel_charge
):
    bond_count = lax.axis_size("bond")
    operator_count = lax.axis_size("op")
    root_count, sector_rows, column_strip = wavefunction.shape
    local_channels = site_operators.shape[0]
    band_rows = sector_rows // bond_count
    first_channel = lax.axis_index("op") * local_channels
    own_charge = lax.dynamic_slice_in_dim(channel_charge, first_channel, local_channels, 0)
    group_width = min(column_strip, B)
    group_count = column_strip // group_width
    site_charge = jnp.array(site_charge_table, dtype=jnp.int32)
    starts = (
        lax.axis_index("bond") * column_strip
        + jnp.arange(group_count, dtype=jnp.int32) * group_width
    )
    classes = (site_charge[starts // M] + right_charge[starts % M // B]) % NQ
    left_order = jnp.argsort(left_charge, stable=True)
    first_class = (own_charge[:, 0][:, None] - classes[None, :]) % NQ
    second_class = jnp.broadcast_to((-classes % NQ)[None, :], first_class.shape)
    right_sources = jax.vmap(block_sources, in_axes=(None, 0))(
        right_charge, -(own_charge[:, 0] + own_charge[:, 1])
    )
    site_matrix = site_masks(site_operators, own_charge)
    sector_psi = wavefunction.astype(jnp.bfloat16).reshape(
        root_count, NPB, B, group_count, group_width
    )
    left_full, right_full = (
        lax.all_gather(left_tiles, "bond", axis=3, tiled=True),
        lax.all_gather(right_tiles, "bond", axis=3, tiled=True),
    )
    first_tiles = pick_left(left_full, left_order, first_class)
    left_side = jnp.einsum(
        "cgmnab,knbgw->ckmagw", first_tiles, sector_psi, preferred_element_type=jnp.float32
    )
    left_side = left_side.astype(jnp.bfloat16).reshape(
        local_channels * root_count, sector_rows, column_strip
    )
    by_rows = lax.all_to_all(left_side, "bond", split_axis=1, concat_axis=2, tiled=True)
    by_rows = by_rows.reshape(local_channels, root_count, band_rows, DP, NB, B)

    def pick_columns(channel_rows, source_index):
        return channel_rows[:, :, :, source_index]

    picked_rows = jax.vmap(pick_columns)(by_rows, right_sources)
    partial_one = right_terms(right_full, picked_rows, site_matrix).sum(axis=0)
    partial_one = partial_one.reshape(root_count, band_rows, DP * M)
    share_width = DP * M // operator_count
    summed = lax.psum(partial_one, "op")
    sigma_one = lax.dynamic_slice_in_dim(summed, lax.axis_index("op") * share_width, share_width, 2)
    rounded_one = summed.astype(jnp.bfloat16)
    rounded_blocks = rounded_one.reshape(root_count, band_rows, DP, NB, B)

    def pick_shared_columns(source_index):
        return rounded_blocks[:, :, :, source_index]

    picked_again = jax.vmap(pick_shared_columns)(right_sources)
    right_side = right_terms(right_full, picked_again, site_matrix)
    right_side = right_side.astype(jnp.bfloat16).reshape(
        local_channels * root_count, band_rows, DP * M
    )
    by_columns = lax.all_to_all(right_side, "bond", split_axis=2, concat_axis=1, tiled=True)
    by_columns = by_columns.reshape(local_channels, root_count, NPB, B, group_count, group_width)
    second_tiles = pick_left(left_full, left_order, second_class)
    partial_two = jnp.einsum(
        "cgmnab,cknbgw->ckmagw", second_tiles, by_columns, preferred_element_type=jnp.float32
    ).sum(axis=0)
    partial_two = partial_two.reshape(root_count, sector_rows, column_strip)
    sigma_two = lax.psum_scatter(partial_two, "op", scatter_dimension=1, tiled=True)
    return (sigma_one, sigma_two)


def solution(mesh):
    return jax.shard_map(
        local,
        mesh=mesh,
        in_specs=(
            P(None, None, "bond"),
            P("op", None, None, "bond", None),
            P("op", None, None, "bond", None),
            P("op", None, None),
            P(),
            P(),
            P(),
        ),
        out_specs=(P(None, "bond", "op"), P(None, "op", "bond")),
        check_vma=False,
    )
```

profile of v0, /device:TPU:0, one launch (start us, length us, event | category | flops | bytes accessed | tf_op | source)
XLA Modules:
  0.0 1425.0 jit_solution(16086372687354315001)
XLA Ops:
  7.2 0.7 all-gather.3.cloned.1.call-update
  8.0 1.3 gather_fusion
  9.3 1.3 gather_fusion.1
  10.6 0.5 fusion.47
  11.3 0.1 reshape.438
  11.4 1.9 sort.34
  13.4 0.8 gather_fusion.2
  14.1 0.1 gather.36
  14.3 0.1 reshape.468
  14.4 2.1 convert_element_type.18
  16.5 0.4 reshape.412
  16.9 138.4 %all-gather.3.cloned.1.call-done = bf16[8,16,2,128,128]{4,3,2,1,0:T(8,128)(2,1)} async-done(((bf16[8,16,2,8,128]{4,3,2,1,0:T(8,128)(2,1)}), bf16[8,16,2,128,128]{4,3,2,1,0:T(8,128)(2,1)}) %all-gather.3.cloned.1.call-update) | async-done | bytes 8388624 | tf_op jit(solution)/shard_map/all_gather | solution.py:77
  155.3 6.4 gather_fusion.6
  161.7 6.9 fusion.10
  168.6 32.3 %copy.103 = bf16[8,6,2,128,4,128]{5,4,1,0,3,2:T(4,128)(2,1)} copy(bf16[8,6,2,128,4,128]{5,3,1,2,0,4:T(8,128)(2,1)S(1)} %fusion.10) | data formatting | bytes 25165824 | tf_op jit(solution)/shard_map/reshape | solution.py:84
  201.0 19.0 %reshape.505 = bf16[48,256,512]{2,0,1:T(8,128)(2,1)} reshape(bf16[8,6,2,128,4,128]{5,4,1,0,3,2:T(4,128)(2,1)} %copy.103) | data formatting | bytes 25165824 | tf_op jit(solution)/shard_map/reshape | solution.py:84
  220.0 5.1 all-to-all-start
  225.1 0.7 all-gather.5.cloned.1.call-update
  225.8 0.2 all-reduce.2.cloned.1.call-start
  226.0 1.2 sort.35
  227.4 0.1 compare_select_fusion.1
  227.5 0.1 reshape.446
  227.6 1.9 gather_fusion.3
  229.5 0.1 gather.39
  229.7 0.1 reshape.474
  229.9 0.1 select_bitcast_fusion
  230.0 272.9 %all-to-all-done = bf16[48,256,512]{2,0,1:T(8,128)(2,1)} async-done(((bf16[48,256,512]{2,0,1:T(8,128)(2,1)}), bf16[48,256,512]{2,0,1:T(8,128)(2,1)}, u32[]{:S(2)}, u32[]{:S(2)}) %all-to-all-start) | async-done | bytes 12582944 | tf_op jit(solution)/shard_map/all_to_all | solution.py:87
  502.9 14.4 %copy.149 = bf16[48,16,16,512]{3,1,2,0:T(8,128)(2,1)} copy(bf16[48,16,16,512]{3,0,2,1:T(8,128)(2,1)} %bitcast.9) | data formatting | bytes 25165824 | tf_op jit(solution)/shard_map/all_to_all | solution.py:87
  517.4 20.3 %reshape.414 = bf16[8,6,16,4,16,128]{5,4,3,2,1,0:T(8,128)(2,1)} reshape(bf16[48,16,16,512]{3,2,1,0:T(8,128)(2,1)} %bitcast.117) | data formatting | bytes 25165824 | tf_op jit(solution)/shard_map/reshape | solution.py:88
  537.6 25.7 %copy.72 = bf16[8,6,16,4,16,128]{5,2,4,3,1,0:T(8,128)(2,1)} copy(bf16[8,6,16,4,16,128]{5,4,3,2,1,0:T(8,128)(2,1)} %reshape.414) | data formatting | bytes 25165824 | tf_op jit(solution)/shard_map/reshape | solution.py:88
  563.4 19.4 %gather_fusion.7 = bf16[256,6,16,4,128]{4,2,3,1,0:T(8,128)(2,1)} fusion(bf16[8,6,16,4,16,128]{5,2,4,3,1,0:T(8,128)(2,1)} %copy.72, s32[256]{0:T(256)S(1)} %reshape.474), kind=kCustom, calls=%fused_computation.7 | custom fusion | bytes 50333696 | tf_op jit(solution)/shard_map/vmap()/gather | solution.py:91
  582.8 6.0 all-gather.5.cloned.1.call-done
  588.7 23.5 %fusion.15 = f32[8,6,16,4,16,128]{5,2,3,1,4,0:T(8,128)} fusion(bf16[8,16,2,6,16,4,128]{6,4,5,3,2,1,0:T(8,128)(2,1)} %bitcast.115, bf16[8,16,2,128,128]{4,3,2,1,0:T(8,128)(2,1)} %all-gather.5.cloned.1.call-done), kind=kOutput, calls=%fused_computation.25 | convolution fusion | flops 3221225472 | bytes 58720256 | tf_op jit(solution)/shard_map/cjnab,ckrpjnb->ckrpja/dot_general | solution.py:42
  612.3 32.9 %fusion.25 = f32[6,16,4,16,128]{4,2,3,1,0:T(4,128)S(1)} fusion(f32[8,6,16,4,16,128]{5,2,3,1,4,0:T(8,128)} %fusion.15, f32[8,4,4,1,1,1]{0,2,1,5,4,3:T(4,128)S(1)} %select_bitcast_fusion), kind=kOutput, calls=%fused_computation.31 | convolution fusion | flops 301989888 | bytes 28312064 | tf_op jit(solution)/shard_map/cpq,ckrqja->ckrpja/dot_general | solution.py:45
  645.2 0.3 copy.76
  645.5 2.4 reshape.415
  647.9 0.1 copy.95
  648.0 0.1 reshape.454
  648.2 131.5 %all-reduce.2.cloned.1.call-done = f32[6,16,8192]{2,1,0:T(8,128)} async-done(((f32[6,16,8192]{2,1,0:T(8,128)}), f32[6,16,8192]{2,1,0:T(8,128)}) %all-reduce.2.cloned.1.call-update) | async-done | bytes 3145744 | tf_op jit(solution)/shard_map/psum | solution.py:97
  779.7 2.1 convert_element_type.21
  781.8 0.4 copy.113
  782.2 1.0 copy.77
  783.2 12.9 gather_fusion.4
  796.1 23.5 %fusion.18 = f32[8,6,16,4,16,128]{5,2,3,1,4,0:T(8,128)} fusion(bf16[8,16,2,6,16,4,128]{6,4,5,3,2,1,0:T(8,128)(2,1)} %bitcast.116, bf16[8,16,2,128,128]{4,3,2,1,0:T(8,128)(2,1)} %all-gather.5.cloned.1.call-done), kind=kOutput, calls=%fused_computation.26 | convolution fusion | flops 3221225472 | bytes 58720256 | tf_op jit(solution)/shard_map/cjnab,ckrpjnb->ckrpja/dot_general | solution.py:42
  819.7 56.9 %convert_bitcast_fusion = bf16[8,6,16,4,16,128]{5,3,4,2,1,0:T(4,128)(2,1)S(1)} fusion(f32[8,4,4,1,1,1]{2,1,5,4,3,0:T(4,128)S(1)} %copy.95, f32[8,6,16,4,16,128]{5,2,3,1,4,0:T(8,128)} %fusion.18), kind=kOutput, calls=%fused_computation.24 | convolution fusion | flops 308281344 | bytes 37749248 | tf_op jit(solution)/shard_map/cpq,ckrqja->ckrpja/dot_general | solution.py:45
  876.6 6.5 copy.81
  883.1 19.3 %reshape.417 = bf16[48,16,8192]{2,1,0:T(8,128)(2,1)} reshape(bf16[8,6,16,4,16,128]{5,4,3,2,1,0:T(8,128)(2,1)} %copy.81) | data formatting | bytes 25165824 | tf_op jit(solution)/shard_map/reshape | solution.py:107
  902.4 47.8 %copy.82 = bf16[48,16,8192]{0,1,2:T(8,128)(2,1)} copy(bf16[48,16,8192]{2,1,0:T(8,128)(2,1)} %reshape.417) | data formatting | bytes 25165824 | tf_op jit(solution)/shard_map/reshape | solution.py:107
  950.2 51.9 %reshape.506 = bf16[16,2,196608]{2,1,0:T(2,128)(2,1)} reshape(bf16[8192,16,48]{2,1,0:T(8,128)(2,1)} %bitcast.113) | data formatting | bytes 25165824
  1002.1 7.0 all-to-all-start.1
  1009.2 0.1 reshape.462
  1009.4 0.8 gather_fusion.5
  1010.2 0.1 gather.43
  1010.3 0.1 reshape.480
  1010.4 6.5 gather_fusion.8
  1016.9 229.9 %all-to-all-done.1 = bf16[16,2,196608]{2,1,0:T(2,128)(2,1)} async-done(((bf16[16,2,196608]{2,1,0:T(2,128)(2,1)}), bf16[16,2,196608]{2,1,0:T(2,128)(2,1)}, u32[]{:S(2)}, u32[]{:S(2)}) %all-to-all-start.1) | async-done | bytes 12582944 | tf_op jit(solution)/shard_map/all_to_all | solution.py:110
  1246.7 33.6 %reshape.507 = bf16[8192,16,48]{2,1,0:T(8,128)(2,1)} reshape(bf16[16,2,196608]{2,1,0:T(2,128)(2,1)} %all-to-all-done.1) | data formatting | bytes 25165824
  1280.3 40.1 %copy.83 = bf16[48,16,16,512]{3,1,2,0:T(8,128)(2,1)} copy(bf16[48,16,16,512]{0,1,3,2:T(8,128)(2,1)} %bitcast.114) | data formatting | bytes 25165824 | tf_op jit(solution)/shard_map/all_to_all | solution.py:110
  1320.4 18.2 %reshape.418 = bf16[8,6,2,128,4,128]{5,4,3,2,1,0:T(4,128)(2,1)} reshape(bf16[48,16,16,512]{3,2,1,0:T(8,128)(2,1)} %bitcast.118) | data formatting | bytes 25165824 | tf_op jit(solution)/shard_map/reshape | solution.py:111
  1338.6 11.7 fusion.28
  1350.2 3.3 copy.86
  1353.5 2.8 reshape.419
  1356.4 2.7 constant_dynamic-slice_fusion
  1359.0 59.2 %reduce-scatter.2.cloned.1.call-done = f32[6,128,512]{2,1,0:T(8,128)} async-done(((f32[6,256,512]{2,1,0:T(8,128)}), f32[6,128,512]{2,1,0:T(8,128)}) %reduce-scatter.2.cloned.1.call-update) | async-done | bytes 1572880 | tf_op jit(solution)/shard_map/reduce_scatter | solution.py:117
  (42 shorter events, 0.8 us)
Async XLA Ops:
  7.2 3.4 copy-start
  7.2 148.1 %all-gather.3.cloned.1.call-start = ((), (), s32[]{:S(2)}) async-start(), calls=%async_computation.3 | async-start | bytes 8912896 | tf_op jit(solution)/shard_map/all_gather | solution.py:77
  13.3 148.3 %copy-start.2 = (s32[16]{0:T(128)}, s32[16]{0:T(128)S(1)}, u32[]{:S(2)}) copy-start(s32[16]{0:T(128)S(1)} %get-tuple-element.4) | copy-start | bytes 196
  220.0 6.1 copy-start.4
  220.0 282.9 %all-to-all-start = ((bf16[48,256,512]{2,0,1:T(8,128)(2,1)}), bf16[48,256,512]{2,0,1:T(8,128)(2,1)}, u32[]{:S(2)}, u32[]{:S(2)}) async-start(bf16[48,256,512]{2,0,1:T(8,128)(2,1)} %reshape.505), calls=%async_computation | async-start | bytes 25165824 | tf_op jit(solution)/shard_map/all_to_all | solution.py:87
  225.0 363.7 %all-gather.5.cloned.1.call-start = ((), (), s32[]{:S(2)}) async-start(), calls=%async_computation.4 | async-start | bytes 8912896 | tf_op jit(solution)/shard_map/all_gather | solution.py:78
  225.8 553.9 %all-reduce.2.cloned.1.call-start = ((), (), s32[]{:S(2)}) async-start(), calls=%async_computation.5 | async-start | bytes 6291456 | tf_op jit(solution)/shard_map/psum | solution.py:97
  227.6 2.2 copy-start.5
  227.6 2.2 copy-start.8
  227.6 2.3 copy-start.6
  1002.1 7.0 copy-start.7
  1002.1 7.3 copy-start.3
  1002.1 244.6 %all-to-all-start.1 = ((bf16[16,2,196608]{2,1,0:T(2,128)(2,1)}), bf16[16,2,196608]{2,1,0:T(2,128)(2,1)}, u32[]{:S(2)}, u32[]{:S(2)}) async-start(bf16[16,2,196608]{2,1,0:T(2,128)(2,1)} %reshape.506), calls=%async_computation.1 | async-start | bytes 25165824 | tf_op jit(solution)/shard_map/all_to_all | solution.py:110
  1009.1 409.1 %reduce-scatter.2.cloned.1.call-start = ((), (), s32[]{:S(2)}) async-start(), calls=%async_computation.6 | async-start | bytes 4718592 | tf_op jit(solution)/shard_map/reduce_scatter | solution.py:117
  1338.6 79.7 %copy-start.1 = (s32[16,2]{0,1:T(2,128)S(1)}, s32[16,2]{0,1:T(2,128)}, u32[]{:S(2)}) copy-start(s32[16,2]{0,1:T(2,128)} %param.15) | copy-start | bytes 388
Sparse Core Ops, SparseCore 0:
  10.7 144.5 all-gather.2
  228.6 360.1 all-gather.4
  648.1 131.6 all-reduce.1
  1356.5 61.7 reduce-scatter.1
where the time goes:
time: 1430 us; the launch traced here: 1420 us
  waiting for transfers between devices  839 us (59%)
  local copies, waits for them, and re-layouts  395 us (28%)
  matrix products  156 us (11%)
  between operations  14.3 us (1%)
    all_to_all x1, waiting for transfers between devices, local(): lax.all_to_all(left_side, 'bond', split_axis=1, concat_axis=2, tiled=True)  273 us
    all_to_all x1, waiting for transfers between devices, local(): lax.all_to_all(right_side, 'bond', split_axis=2, concat_axis=1, tiled=True)  230 us
    all_gather x1, waiting for transfers between devices, local(): lax.all_gather(left_tiles, 'bond', axis=3, tiled=True)  138 us
    psum x1, waiting for transfers between devices, local(): summed = lax.psum(partial_one, 'op')  132 us
    dot_general x2, matrix products, right_terms(): jnp.einsum('cpq,ckrqja->ckrpja', site_matrix, inner_sum, precision=lax.Pr...  89.8 us
    unnamed x21, local copies, waits for them, and re-layouts  86 us
    reshape x2, local copies, waits for them, and re-layouts, local(): right_side.astype(jnp.bfloat16)  67 us
    reduce_scatter x1, waiting for transfers between devices, local(): lax.psum_scatter(partial_two, 'op', scatter_dimension=1, tiled=True)  59.2 us
  transfers between devices with their start and end apart: 6, of which 6 were waited for; matrix products, arithmetic and copies ran while one was open for 7% of the time, Pallas kernels for 0%

commit v1 on v0

v1 whole, which is shorter than its diff:
```python
import functools

import jax
import jax.numpy as jnp
from jax import lax
from jax.experimental import pallas as pl
from jax.experimental.pallas import tpu as pltpu
from jax.sharding import PartitionSpec as P

M = 2048
B = 128
NQ = 8
DP = 4
NB = 16
NPB = 2

site_charge_table = (0, 1, 1, 2)
MESH = pl.DeviceIdType.MESH


def site_masks(site_operators, channel_charge):
    site_charge = jnp.array(site_charge_table, dtype=jnp.int32)
    charge_step = site_charge[:, None] - site_charge[None, :]
    allowed = (charge_step[None, :, :] - channel_charge[:, 1][:, None, None]) % NQ == 0
    return jnp.where(allowed, site_operators, jnp.zeros_like(site_operators))


def spread_kernel(half, ops, x_ref, g_ref, own_sem, send_sem, recv_sem, fsend, frecv):
    bond = lax.axis_index("bond")
    o = lax.axis_index("op")
    i = lax.rem(bond, half)
    base = bond - i

    barrier = pltpu.get_barrier_semaphore()
    for d in range(1, half):
        pl.semaphore_signal(
            barrier, inc=1, device_id={"bond": base + lax.rem(i + d, half), "op": o},
            device_id_type=MESH,
        )
    for e in range(1, ops):
        pl.semaphore_signal(
            barrier, inc=1, device_id={"bond": bond, "op": lax.rem(o + e, ops)},
            device_id_type=MESH,
        )
    pl.semaphore_wait(barrier, half - 1 + ops - 1)

    copies = []
    for d in range(1, half):
        copy = pltpu.make_async_remote_copy(
            src_ref=x_ref, dst_ref=g_ref.at[i, o], send_sem=send_sem.at[d], recv_sem=recv_sem.at[d],
            device_id={"bond": base + lax.rem(i + d, half), "op": o}, device_id_type=MESH,
        )
        copy.start()
        copies.append(copy)

    def forward(d, src, slot):
        sent = []
        for e in range(1, ops):
            copy = pltpu.make_async_remote_copy(
                src_ref=src, dst_ref=g_ref.at[slot, o],
                send_sem=fsend.at[d, e], recv_sem=frecv.at[d, e],
                device_id={"bond": bond, "op": lax.rem(o + e, ops)}, device_id_type=MESH,
            )
            copy.start()
            sent.append(copy)
        return sent

    forwards = forward(0, x_ref, i)
    own = pltpu.make_async_copy(x_ref, g_ref.at[i, o], own_sem)
    own.start()
    for d in range(1, half):
        copies[d - 1].wait_recv()
        slot = lax.rem(i - d + half, half)
        forwards += forward(d, g_ref.at[slot, o], slot)
    own.wait()
    for copy in copies:
        copy.wait_send()
    for copy in forwards:
        copy.wait()


def spread(x, half, ops, collective_id):
    return pl.pallas_call(
        functools.partial(spread_kernel, half, ops),
        out_shape=jax.ShapeDtypeStruct((half, ops) + x.shape, x.dtype),
        in_specs=[pl.BlockSpec(memory_space=pltpu.VMEM)],
        out_specs=pl.BlockSpec(memory_space=pl.ANY),
        scratch_shapes=[
            pltpu.SemaphoreType.DMA,
            pltpu.SemaphoreType.DMA((half,)),
            pltpu.SemaphoreType.DMA((half,)),
            pltpu.SemaphoreType.DMA((half, ops)),
            pltpu.SemaphoreType.DMA((half, ops)),
        ],
        compiler_params=pltpu.CompilerParams(collective_id=collective_id, has_side_effects=True),
        name=f"spread_{collective_id}",
    )(x)


def apply_kernel(
    channels, rows, roots, site_charges,
    order_ref, shift_ref, site_ref, psi_ref, left_ref, right_ref, out_ref, mixed
):
    @pl.loop(0, NQ)
    def _(g):
        for n in range(NPB):
            r = order_ref[g * NPB + n]
            terms = []
            for q in range(DP):
                h = lax.rem(2 * NQ - site_charges[q] - g, NQ)
                terms.append(
                    jnp.dot(left_ref[h], psi_ref[q * NB + r], preferred_element_type=jnp.float32)
                )
            for c in range(channels):
                for p in range(DP):
                    total = site_ref[(c * DP + p) * DP] * terms[0][c * rows:(c + 1) * rows]
                    for q in range(1, DP):
                        total += site_ref[(c * DP + p) * DP + q] * terms[q][c * rows:(c + 1) * rows]
                    total = total.astype(jnp.bfloat16)
                    for k in range(roots):
                        at = (p * roots + k) * rows
                        mixed[c, g, at:at + rows, n * B:(n + 1) * B] = total[:, k * B:(k + 1) * B]

    @pl.loop(0, NQ)
    def _(g):
        total = None
        for c in range(channels):
            source = lax.rem(g + shift_ref[c], NQ)
            term = lax.dot_general(
                mixed[c, source], right_ref[c, g], (((1,), (1,)), ((), ())),
                preferred_element_type=jnp.float32,
            )
            total = term if total is None else total + term
        for m in range(NPB):
            out_ref[order_ref[g * NPB + m]] = total[:, m * B:(m + 1) * B]


def apply_all(order, shift, site, psi, left, right, rows, roots):
    channels = right.shape[0]
    height = DP * roots * rows
    smem = pl.BlockSpec(memory_space=pltpu.SMEM)
    vmem = pl.BlockSpec(memory_space=pltpu.VMEM)
    return pl.pallas_call(
        functools.partial(apply_kernel, channels, rows, roots, site_charge_table),
        out_shape=jax.ShapeDtypeStruct((NB, height, B), jnp.float32),
        in_specs=[smem, smem, smem, vmem, vmem, vmem],
        out_specs=vmem,
        scratch_shapes=[pltpu.VMEM((channels, NQ, height, NPB * B), jnp.bfloat16)],
        compiler_params=pltpu.CompilerParams(vmem_limit_bytes=58 * 1024 * 1024),
        name="apply_all",
    )(order, shift, site, psi, left, right)


def local(
    wavefunction, left_tiles, right_tiles, site_operators, left_charge, right_charge, channel_charge
):
    bonds = lax.axis_size("bond")
    ops = lax.axis_size("op")
    bond = lax.axis_index("bond")
    op = lax.axis_index("op")
    roots, sector_rows, strip = wavefunction.shape
    channels = site_operators.shape[0]
    half = bonds // 2
    part = bond // half
    some = roots // 2
    chunk = left_tiles.shape[3]
    band = 2 * chunk
    rows = NPB * band
    held = -(-rows // 16) * 16
    width = min(strip, B)
    groups = strip // width
    own_charge = lax.dynamic_slice_in_dim(channel_charge, op * channels, channels, 0)
    left_order = jnp.argsort(left_charge, stable=True).astype(jnp.int32)
    right_order = jnp.argsort(right_charge, stable=True).astype(jnp.int32)
    shift = (own_charge[:, 0] + own_charge[:, 1]) % NQ
    site = site_masks(site_operators, own_charge).reshape(-1)
    partner = [(b, (b + half) % bonds) for b in range(bonds)]

    right = right_tiles[:, right_order].transpose(0, 1, 3, 2, 4).reshape(
        channels, NB, chunk, NPB * B
    )
    right = lax.all_gather(right, "bond", axis=2, tiled=True).reshape(
        channels, NQ, NPB * B, NPB * B
    )

    even = [(b, b // 2 + (b % 2) * half) for b in range(bonds)]
    odd = [(b, b // 2 + (1 - b % 2) * half) for b in range(bonds)]
    one = lax.ppermute(left_tiles, "bond", even)
    two = lax.ppermute(left_tiles, "bond", odd)
    low = jnp.where(part == 0, one, two)
    high = jnp.where(part == 0, two, one)
    left = jnp.concatenate([low, high], axis=3)
    left_slots = ((jnp.arange(NQ)[:, None] + own_charge[None, :, 0]) % NQ)[:, :, None] * NPB + jnp.arange(NPB)
    left = left[jnp.arange(channels)[None, :, None], left_order[left_slots]]
    left = left.transpose(0, 1, 2, 4, 3, 5).reshape(NQ, channels, rows, NPB * B)
    left = jnp.pad(left, ((0, 0), (0, 0), (0, held - rows), (0, 0)))
    left = left.reshape(NQ, channels * held, NPB * B)

    share = sector_rows // ops
    psi = lax.dynamic_slice_in_dim(wavefunction, op * share, share, 1).astype(jnp.bfloat16)
    psi = psi.reshape(2, some, share, groups, width).transpose(0, 3, 2, 1, 4)
    psi = psi.reshape(2, groups, share, some * width)
    kept = lax.dynamic_index_in_dim(psi, part, 0, keepdims=False)
    came = lax.ppermute(lax.dynamic_index_in_dim(psi, 1 - part, 0, keepdims=False), "bond", partner)
    piece = jnp.stack([jnp.where(part == 0, kept, came), jnp.where(part == 0, came, kept)])
    gathered = spread(piece, half, ops, 1)
    if width == B:
        psi = gathered.transpose(2, 0, 3, 1, 4, 5).reshape(DP * NB, sector_rows, some * B)
    else:
        psi = gathered.reshape(half, ops, 2, share, some, strip).transpose(2, 0, 5, 1, 3, 4)
        psi = psi.reshape(DP * NB, B, sector_rows, some).transpose(0, 2, 3, 1)
        psi = psi.reshape(DP * NB, sector_rows, some * B)

    def unpack(result):
        result = result.reshape(NB, DP, some, held, B)[:, :, :, :rows]
        return result.reshape(NB, DP, some, NPB, band, B)

    def summed_share(parts, axis):
        size = parts.shape[axis] // ops
        total = lax.dynamic_slice_in_dim(parts, op * size, size, axis)
        for e in range(1, ops):
            to = (op + e) % ops
            sent = lax.dynamic_slice_in_dim(parts, to * size, size, axis)
            total += lax.ppermute(sent, "op", [(o, (o + e) % ops) for o in range(ops)])
        return total

    first = unpack(apply_all(right_order, shift, site, psi, left, right, held, some))
    turned = (DP * NB, some, NPB, band, B)
    if DP % ops == 0:
        first = summed_share(first, 1).transpose(1, 0, 2, 3, 4, 5)
        first = first.reshape((DP * NB // ops,) + turned[1:])
    else:
        first = summed_share(first.transpose(1, 0, 2, 3, 4, 5).reshape(turned), 0)
    blocks = first.shape[0]

    mine = lax.dynamic_index_in_dim(first, part, 2, keepdims=False)
    theirs = lax.dynamic_index_in_dim(first, 1 - part, 2, keepdims=False)
    back = lax.ppermute(theirs.astype(jnp.bfloat16), "bond", partner).astype(jnp.float32)
    both = jnp.stack([jnp.where(part == 0, mine, back), jnp.where(part == 0, back, mine)])
    sigma_one = both.transpose(0, 2, 3, 1, 4).reshape(roots, band, blocks * B)

    again = first.astype(jnp.bfloat16).transpose(0, 2, 3, 1, 4)
    again = again.reshape(blocks, NPB, band, some * B)
    again = spread(again, half, ops, 2)
    again = again.transpose(1, 2, 3, 0, 4, 5).reshape(DP * NB, sector_rows, some * B)
    second = unpack(apply_all(right_order, shift, site, again, left, right, held, some))
    if ops == NPB:
        second = summed_share(second, 3)
    else:
        second = lax.psum(second, "op")
    tiles = second.shape[3]
    second = second.astype(jnp.bfloat16).transpose(2, 3, 4, 1, 0, 5)
    second = second.reshape(some, tiles * band, bonds, strip).transpose(2, 0, 1, 3)
    second = lax.all_to_all(second, "bond", split_axis=0, concat_axis=0, tiled=True)
    second = second.reshape(2, half, some, tiles, band, strip).transpose(0, 2, 3, 1, 4, 5)
    second = second.reshape(roots, tiles * B, strip).astype(jnp.float32)
    if ops != NPB:
        second = lax.dynamic_slice_in_dim(second, op * share, share, 1)
    return (sigma_one, second)


def solution(mesh):
    return jax.shard_map(
        local,
        mesh=mesh,
        in_specs=(
            P(None, None, "bond"),
            P("op", None, None, "bond", None),
            P("op", None, None, "bond", None),
            P("op", None, None),
            P(),
            P(),
            P(),
        ),
        out_specs=(P(None, "bond", "op"), P(None, "op", "bond")),
        check_vma=False,
    )
```

time: 1430 us -> 512 us (0.36)
  waiting for transfers between devices: 839 us -> 92.3 us
  local copies, waits for them, and re-layouts: 395 us -> 52 us
  Pallas kernels: 0 us -> 310 us
  matrix products: 156 us -> 0 us
  starting transfers between devices: 12.4 us -> 28.3 us
    all_to_all x2 -> x1, waiting for transfers between devices: 503 us -> 0.01 us  [local(): lax.all_to_all(second, 'bond', split_axis=0, concat_axis=0, tiled=True)]
    pallas_call x0 -> x4, Pallas kernels: none -> 310 us  [the longest x2 261 us: spread(): pl.pallas_call(functools.partial(spread_kernel, half, ops), out_shape=jax...]
    reshape x11 -> x6, local copies, waits for them, and re-layouts: 189 us -> 8.44 us  [the longest x1 1.89 us: local(): right_tiles[:, right_order].transpose(0, 1, 3, 2, 4)]
    dot_general x6 -> x0, matrix products: 156 us -> none  [the longest x2 89.8 us: right_terms(): jnp.einsum('cpq,ckrqja->ckrpja', site_matrix, inner_sum, precision=lax.Pr...]
    all_gather x2 -> x1, waiting for transfers between devices: 144 us -> 0.01 us  [local(): lax.all_gather(right, 'bond', axis=2, tiled=True)]
    psum x1 -> x0, waiting for transfers between devices: 132 us -> none  [local(): summed = lax.psum(partial_one, 'op')]
    ppermute x0 -> x6, waiting for transfers between devices: none -> 92.3 us  [the longest x1 45.2 us: local(): lax.ppermute(lax.dynamic_index_in_dim(psi, 1 - part, 0, keepdims=False),...]
    unnamed x21 -> x20, local copies, waits for them, and re-layouts: 86 us -> 2.67 us
  transfers between devices with their start and end apart: 6 -> 8, of which waited for: 6 -> 4; matrix products, arithmetic and copies ran while one was open for 7% -> 6% of each run, Pallas kernels for 0% -> 26%
where the time goes in v1:
time: 512 us; the launch traced here: 511 us
  Pallas kernels  310 us (61%)
  waiting for transfers between devices  92.3 us (18%)
  local copies, waits for them, and re-layouts  52 us (10%)
  starting transfers between devices  28.3 us (6%)
  between operations  14.4 us (3%)
  other arithmetic  13.9 us (3%)
    pallas_call x2, Pallas kernels, spread(): pl.pallas_call(functools.partial(spread_kernel, half, ops), out_shape=jax...  261 us
    pallas_call x2, Pallas kernels, apply_all(): pl.pallas_call(functools.partial(apply_kernel, channels, rows, roots, sit...  49.3 us
    ppermute x1, waiting for transfers between devices, local(): lax.ppermute(lax.dynamic_index_in_dim(psi, 1 - part, 0, keepdims=False),...  45.2 us
    ppermute x1, waiting for transfers between devices, local(): lax.ppermute(theirs.astype(jnp.bfloat16), 'bond', partner)  39.9 us
    all_to_all x1, starting transfers between devices, local(): lax.all_to_all(second, 'bond', split_axis=0, concat_axis=0, tiled=True)  15.8 us
    transpose x1, local copies, waits for them, and re-layouts, local(): again.transpose(1, 2, 3, 0, 4, 5).reshape(DP * NB, sector_rows, some * B)  11.8 us
    transpose x1, local copies, waits for them, and re-layouts, local(): gathered.transpose(2, 0, 3, 1, 4, 5).reshape(DP * NB, sector_rows, some * B)  10.9 us
  transfers between devices with their start and end apart: 8, of which 4 were waited for; matrix products, arithmetic and copies ran while one was open for 6% of the time, Pallas kernels for 26%

profile of v1, /device:TPU:0, one launch (start us, length us, event | category | flops | bytes accessed | tf_op | source)
XLA Modules:
  0.0 510.7 jit_solution(10388946068283236289)
XLA Ops:
  7.2 0.0 all-gather.2.cloned.1.call-start
  7.2 2.0 sort.31
  9.3 2.5 gather_fusion.2
  11.8 1.9 copy_bitcast_fusion.1
  13.7 0.0 all-gather.2.cloned.1.call-update
  13.7 4.1 collective-permute-start.2
  17.8 5.4 %collective-permute-start.1 = (bf16[8,16,2,8,128]{4,3,2,1,0:T(8,128)(2,1)}, bf16[8,16,2,8,128]{4,3,2,1,0:T(8,128)(2,1)}, u32[]{:S(2)}, u32[]{:S(2)}) collective-permute-start(bf16[8,16,2,8,128]{4,3,2,1,0:T(8,128)(2,1)} %param.9), channel_id=1, source_target_pairs={{0,0},{2,16},{4,2},{6,18},{8,4},{10,20},{12,6},{14,22},{16,8},{18,... | collective-permute-start | bytes 1572872 | tf_op jit(solution)/shard_map/ppermute | solution.py:188
  23.2 1.0 constant_dynamic-slice_fusion.5
  24.2 1.6 copy.58
  25.8 0.1 copy.45
  25.9 0.1 constant_dynamic-slice_fusion.4
  26.0 0.2 copy.47
  26.2 0.1 collective-permute-start
  26.3 0.1 copy-done.5
  26.4 0.1 constant_dynamic-slice_fusion.6
  26.5 0.1 broadcast_add_fusion
  26.6 0.1 fusion.12
  26.7 0.1 copy.43
  26.8 0.6 reshape.141.site_ref
  27.4 0.1 compare_select_fusion.1
  27.5 0.1 reshape.157
  27.7 1.2 sort.32
  28.9 1.2 gather_fusion
  30.1 0.1 gather.12
  30.3 0.1 reshape.163
  30.4 0.2 copy.46
  30.7 0.5 and_select_fusion.shift_ref
  31.2 45.2 %collective-permute-done = bf16[4,128,384]{2,1,0:T(8,128)(2,1)S(1)} collective-permute-done((bf16[4,128,384]{2,1,0:T(8,128)(2,1)S(1)}, bf16[4,128,384]{2,1,0:T(8,128)(2,1)S(1)}, u32[]{:S(2)}, u32[]{:S(2)}) %collective-permute-start) | collective-permute-done | bytes 393248 | tf_op jit(solution)/shard_map/ppermute | solution.py:204
  76.4 0.1 fusion.5
  76.5 1.0 pad_maximum_fusion.1.x_ref
  77.5 132.9 %spread_1.1 = bf16[8,2,2,4,128,384]{5,4,3,2,1,0:T(8,128)(2,1)} custom-call(bf16[2,4,128,384]{3,2,1,0:T(8,128)(2,1)} %pad_maximum_fusion.1.x_ref), custom_call_target="tpu_custom_call" | custom-call | tf_op jit(solution)/shard_map/spread_1/pallas_call | solution.py:83
  210.3 10.9 %copy.48 = bf16[2,8,4,2,128,384]{5,4,3,2,1,0:T(8,128)(2,1)} copy(bf16[2,8,4,2,128,384]{5,4,2,0,3,1:T(8,128)(2,1)} %bitcast.79) | data formatting | bytes 25165824 | tf_op jit(solution)/shard_map/transpose | solution.py:208
  221.2 1.3 broadcast_select_fusion.1
  222.5 0.2 pad_maximum_fusion
  222.7 0.9 gather_fusion.1
  223.7 1.2 copy.68
  224.8 1.5 reshape.145.left_ref
  226.3 24.5 %apply_all.2 = f32[16,384,128]{2,1,0:T(8,128)} custom-call(s32[16]{0:T(128)} %copy-done.4, s32[8]{0:T(128)} %and_select_fusion.shift_ref, f32[128]{0:T(128)} %reshape.141.site_ref, bf16[64,256,384]{2,1,0:T(8,128)(2,1)} %bitcast.81, bf16[8,256,256]{2,1,0:T(8,128)(2,1)} %reshape.145.left_ref, bf16[8,8,256,256]{3,2,1,0:T(8,128)(2,1)} %bitcast.83), custom_call_target="tpu_custom_call" | custom-call | tf_op jit(solution)/shard_map/apply_all/pallas_call | solution.py:143
  250.9 2.9 constant_dynamic-slice_fusion.2
  253.8 3.7 collective-permute-done.3
  257.5 1.8 add_bitcast_fusion
  259.3 1.3 copy.51
  260.5 0.6 convert_bitcast_fusion.1
  261.1 1.4 reshape.150.x_ref
  262.6 127.7 %spread_2.1 = bf16[8,2,32,2,16,384]{5,4,3,2,1,0:T(8,128)(2,1)} custom-call(bf16[32,2,16,384]{3,2,1,0:T(8,128)(2,1)} %reshape.150.x_ref), custom_call_target="tpu_custom_call" | custom-call | tf_op jit(solution)/shard_map/spread_2/pallas_call | solution.py:83
  390.3 11.8 %copy.53 = bf16[2,32,2,8,16,384]{5,4,3,2,1,0:T(8,128)(2,1)} copy(bf16[2,32,2,8,16,384]{5,4,2,1,0,3:T(8,128)(2,1)} %bitcast.80) | data formatting | bytes 25165824 | tf_op jit(solution)/shard_map/transpose | solution.py:245
  402.1 24.7 %apply_all.3 = f32[16,384,128]{2,1,0:T(8,128)} custom-call(s32[16]{0:T(128)} %copy-done.4, s32[8]{0:T(128)} %and_select_fusion.shift_ref, f32[128]{0:T(128)} %reshape.141.site_ref, bf16[64,256,384]{2,1,0:T(8,128)(2,1)} %bitcast.82, bf16[8,256,256]{2,1,0:T(8,128)(2,1)} %reshape.145.left_ref, bf16[8,8,256,256]{3,2,1,0:T(8,128)(2,1)} %bitcast.84), custom_call_target="tpu_custom_call" | custom-call | tf_op jit(solution)/shard_map/apply_all/pallas_call | solution.py:143
  426.9 2.2 constant_dynamic-slice_fusion.1
  429.1 0.9 copy.60
  430.1 0.1 collective-permute-start.5
  430.1 3.4 collective-permute-done.5
  433.5 1.9 fusion.3
  435.4 1.6 reshape.152
  437.0 1.3 copy.56
  438.3 15.8 %all-to-all-start = ((bf16[16,3,16,512]{3,2,1,0:T(8,128)(2,1)}), bf16[16,3,16,512]{3,2,1,0:T(8,128)(2,1)}, u32[]{:S(2)}, u32[]{:S(2)}) async-start(bf16[16,3,16,512]{3,2,1,0:T(8,128)(2,1)} %copy.56), calls=%async_computation | async-start | bytes 1572864 | tf_op jit(solution)/shard_map/all_to_all | solution.py:254
  454.1 0.2 fusion.4
  454.4 2.8 collective-permute-start.4
  457.2 39.9 %collective-permute-done.4 = bf16[32,3,16,128]{3,1,2,0:T(4,128)(2,1)S(1)} collective-permute-done((bf16[32,3,16,128]{3,1,2,0:T(4,128)(2,1)S(1)}, bf16[32,3,16,128]{3,1,2,0:T(4,128)(2,1)S(1)}, u32[]{:S(2)}, u32[]{:S(2)}) %collective-permute-start.4) | collective-permute-done | bytes 393248 | tf_op jit(solution)/shard_map/ppermute | solution.py:238
  497.1 0.6 fusion.1
  497.7 1.0 maximum_bitcast_fusion
  498.7 0.9 copy.52
  499.7 1.4 reshape.149
  501.1 1.5 convert_bitcast_fusion
  502.6 1.3 copy.57
  (30 shorter events, 0.1 us)
Async XLA Ops:
  7.2 16.0 %copy-start = (f32[6,256,512]{2,1,0:T(8,128)S(1)}, f32[6,256,512]{2,1,0:T(8,128)}, u32[]{:S(2)}) copy-start(f32[6,256,512]{2,1,0:T(8,128)} %param.8) | copy-start | bytes 9437188
  7.2 219.1 %all-gather.2.cloned.1.call-start = ((), (), s32[]{:S(2)}) async-start(), calls=%async_computation.1 | async-start | bytes 8912896 | tf_op jit(solution)/shard_map/all_gather | solution.py:182
  9.3 14.9 %copy-start.4 = (s32[16]{0:T(128)}, s32[16]{0:T(128)S(1)}, u32[]{:S(2)}) copy-start(s32[16]{0:T(128)S(1)} %get-tuple-element.4.order_ref) | copy-start | bytes 196
  13.7 207.6 %collective-permute-start.2 = (bf16[8,16,2,8,128]{4,3,2,1,0:T(8,128)(2,1)}, bf16[8,16,2,8,128]{4,3,2,1,0:T(8,128)(2,1)}, u32[]{:S(2)}, u32[]{:S(2)}) collective-permute-start(bf16[8,16,2,8,128]{4,3,2,1,0:T(8,128)(2,1)} %param.9), channel_id=1, source_target_pairs={{0,16},{2,0},{4,18},{6,2},{8,20},{10,4},{12,22},{14,6},{16,24},{18... | collective-permute-start | bytes 1572872 | tf_op jit(solution)/shard_map/ppermute | solution.py:189
  17.8 203.4 %collective-permute-start.1 = (bf16[8,16,2,8,128]{4,3,2,1,0:T(8,128)(2,1)}, bf16[8,16,2,8,128]{4,3,2,1,0:T(8,128)(2,1)}, u32[]{:S(2)}, u32[]{:S(2)}) collective-permute-start(bf16[8,16,2,8,128]{4,3,2,1,0:T(8,128)(2,1)} %param.9), channel_id=1, source_target_pairs={{0,0},{2,16},{4,2},{6,18},{8,4},{10,20},{12,6},{14,22},{16,8},{18,... | collective-permute-start | bytes 1572872 | tf_op jit(solution)/shard_map/ppermute | solution.py:188
  25.7 0.7 copy-start.5
  25.8 0.8 copy-start.6
  25.8 0.7 copy-start.7
  25.8 0.8 copy-start.3
  25.8 1.9 copy-start.8
  26.2 50.2 %collective-permute-start = (bf16[4,128,384]{2,1,0:T(8,128)(2,1)S(1)}, bf16[4,128,384]{2,1,0:T(8,128)(2,1)S(1)}, u32[]{:S(2)}, u32[]{:S(2)}) collective-permute-start(bf16[4,128,384]{2,1,0:T(8,128)(2,1)S(1)} %bitcast.96), channel_id=1, source_target_pairs={{0,16},{2,18},{4,20},{6,22},{8,24},{10,26},{12,28},{14,30},{16,0},... | collective-permute-start | bytes 1179656 | tf_op jit(solution)/shard_map/ppermute | solution.py:204
  250.9 6.6 %copy-start.2 = (f32[16,384,128]{2,1,0:T(8,128)S(1)}, f32[16,384,128]{2,1,0:T(8,128)}, u32[]{:S(2)}) copy-start(f32[16,384,128]{2,1,0:T(8,128)} %apply_all.2) | copy-start | bytes 9437188
  253.8 3.8 collective-permute-start.3
  430.1 3.5 collective-permute-start.5
  438.3 62.8 %all-to-all-start = ((bf16[16,3,16,512]{3,2,1,0:T(8,128)(2,1)}), bf16[16,3,16,512]{3,2,1,0:T(8,128)(2,1)}, u32[]{:S(2)}, u32[]{:S(2)}) async-start(bf16[16,3,16,512]{3,2,1,0:T(8,128)(2,1)} %copy.56), calls=%async_computation | async-start | bytes 1572864 | tf_op jit(solution)/shard_map/all_to_all | solution.py:254
  454.4 42.8 %collective-permute-start.4 = (bf16[32,3,16,128]{3,1,2,0:T(4,128)(2,1)S(1)}, bf16[32,3,16,128]{3,1,2,0:T(4,128)(2,1)S(1)}, u32[]{:S(2)}, u32[]{:S(2)}) collective-permute-start(bf16[32,3,16,128]{3,1,2,0:T(4,128)(2,1)S(1)} %fusion.4), channel_id=1, source_target_pairs={{0,16},{2,18},{4,20},{6,22},{8,24},{10,26},{12,28},{14,30},{16,0},... | collective-permute-start | bytes 1179656 | tf_op jit(solution)/shard_map/ppermute | solution.py:238
  501.1 2.8 copy-start.1
Sparse Core Ops, SparseCore 0:
  13.8 212.0 all-gather.1

commit v2 on v1

--- a/solution.py
+++ b/solution.py
@@ -25,80 +25,149 @@
     return jnp.where(allowed, site_operators, jnp.zeros_like(site_operators))
 
 
-def spread_kernel(half, ops, x_ref, g_ref, own_sem, send_sem, recv_sem, fsend, frecv):
+def spread_kernel(half, ops, colours, first, *refs):
+    if first:
+        x_ref, y_ref, g_ref = refs[:3]
+        z_ref = None
+        scratch = refs[3:]
+    else:
+        x_ref, y_ref, g_ref, z_ref = refs[:4]
+        scratch = refs[4:]
+    own_sem, psend, precv, send_sem, recv_sem, fsend, frecv = scratch
     bond = lax.axis_index("bond")
     o = lax.axis_index("op")
     i = lax.rem(bond, half)
+    part = bond // half
     base = bond - i
+    partner = i + half * (1 - part)
+    bits = half.bit_length() - 1
+    streams = 2 if first else 1
+
+    def place(mask):
+        at = i
+        for t in range(bits):
+            if mask >> t & 1:
+                at = at + (1 << t) * (1 - 2 * lax.rem(i // (1 << t), 2))
+        return at
+
+    def to(bond_index, op_index):
+        return {"bond": bond_index, "op": op_index}
 
     barrier = pltpu.get_barrier_semaphore()
-    for d in range(1, half):
+    for t in range(bits):
         pl.semaphore_signal(
-            barrier, inc=1, device_id={"bond": base + lax.rem(i + d, half), "op": o},
-            device_id_type=MESH,
+            barrier, inc=1, device_id=to(base + place(1 << t), o), device_id_type=MESH
         )
+    pl.semaphore_signal(barrier, inc=1, device_id=to(partner, o), device_id_type=MESH)
     for e in range(1, ops):
         pl.semaphore_signal(
-            barrier, inc=1, device_id={"bond": bond, "op": lax.rem(o + e, ops)},
-            device_id_type=MESH,
+            barrier, inc=1, device_id=to(bond, lax.rem(o + e, ops)), device_id_type=MESH
         )
-    pl.semaphore_wait(barrier, half - 1 + ops - 1)
-
-    copies = []
-    for d in range(1, half):
-        copy = pltpu.make_async_remote_copy(
-            src_ref=x_ref, dst_ref=g_ref.at[i, o], send_sem=send_sem.at[d], recv_sem=recv_sem.at[d],
-            device_id={"bond": base + lax.rem(i + d, half), "op": o}, device_id_type=MESH,
-        )
-        copy.start()
-        copies.append(copy)
-
-    def forward(d, src, slot):
-        sent = []
+    pl.semaphore_wait(barrier, bits + ops)
+
+    index = (part, 1 - part) if first else (0,)
+    exchange = []
+    for c in range(colours if first else 1):
+        exchange.append(pltpu.make_async_remote_copy(
+            src_ref=y_ref.at[c] if first else y_ref,
+            dst_ref=g_ref.at[i, o, part, c] if first else z_ref,
+            send_sem=psend.at[c], recv_sem=precv.at[c],
+            device_id=to(partner, o), device_id_type=MESH,
+        ))
+        exchange[-1].start()
+
+    copies = {}
+    forwards = []
+    ready = set()
+
+    def block(s, c, mask):
+        if s == 0 and mask == 0:
+            return x_ref.at[c]
+        return g_ref.at[place(mask), o, index[s], c]
+
+    def ensure(s, c, mask):
+        if (s, c, mask) in ready:
+            return
+        ready.add((s, c, mask))
+        if mask:
+            copies[s, c, mask].wait_recv()
+        elif s == 1:
+            exchange[c].wait_recv()
         for e in range(1, ops):
             copy = pltpu.make_async_remote_copy(
-                src_ref=src, dst_ref=g_ref.at[slot, o],
-                send_sem=fsend.at[d, e], recv_sem=frecv.at[d, e],
-                device_id={"bond": bond, "op": lax.rem(o + e, ops)}, device_id_type=MESH,
+                src_ref=block(s, c, mask), dst_ref=g_ref.at[place(mask), o, index[s], c],
+                send_sem=fsend.at[s, c, mask, e], recv_sem=frecv.at[s, c, mask, e],
+                device_id=to(bond, lax.rem(o + e, ops)), device_id_type=MESH,
             )
             copy.start()
-            sent.append(copy)
-        return sent
-
-    forwards = forward(0, x_ref, i)
-    own = pltpu.make_async_copy(x_ref, g_ref.at[i, o], own_sem)
+            forwards.append(copy)
+
+    own = pltpu.make_async_copy(x_ref, g_ref.at[i, o, index[0]], own_sem)
     own.start()
-    for d in range(1, half):
-        copies[d - 1].wait_recv()
-        slot = lax.rem(i - d + half, half)
-        forwards += forward(d, g_ref.at[slot, o], slot)
+    for s in range(streams):
+        reached = [[0] for c in range(colours)]
+        for step in range(bits):
+            for at in range(max(len(r) for r in reached)):
+                for c in range(colours):
+                    mask = reached[c][at]
+                    bit = 1 << (c + step) % bits
+                    ensure(s, c, mask)
+                    copy = pltpu.make_async_remote_copy(
+                        src_ref=block(s, c, mask), dst_ref=g_ref.at[place(mask), o, index[s], c],
+                        send_sem=send_sem.at[s, c, mask | bit], recv_sem=recv_sem.at[s, c, mask | bit],
+                        device_id=to(base + place(bit), o), device_id_type=MESH,
+                    )
+                    copy.start()
+                    copies[s, c, mask | bit] = copy
+            for c in range(colours):
+                bit = 1 << (c + step) % bits
+                reached[c] = reached[c] + [mask | bit for mask in reached[c]]
+    for s in range(streams):
+        for mask in range(half):
+            for c in range(colours):
+                ensure(s, c, mask)
     own.wait()
-    for copy in copies:
+    for copy in copies.values():
         copy.wait_send()
+    for copy in exchange:
+        copy.wait_send()
+        if not first:
+            copy.wait_recv()
     for copy in forwards:
         copy.wait()
 
 
-def spread(x, half, ops, collective_id):
+def spread(x, y, half, ops, first):
+    colours = x.shape[0]
+    streams = 2 if first else 1
+    shapes = [jax.ShapeDtypeStruct((half, ops, streams) + x.shape, x.dtype)]
+    if not first:
+        shapes.append(jax.ShapeDtypeStruct(y.shape, y.dtype))
+    size = x.size * half * ops * streams * 2
     return pl.pallas_call(
-        functools.partial(spread_kernel, half, ops),
-        out_shape=jax.ShapeDtypeStruct((half, ops) + x.shape, x.dtype),
-        in_specs=[pl.BlockSpec(memory_space=pltpu.VMEM)],
-        out_specs=pl.BlockSpec(memory_space=pl.ANY),
+        functools.partial(spread_kernel, half, ops, colours, first),
+        out_shape=shapes,
+        in_specs=[pl.BlockSpec(memory_space=pltpu.VMEM)] * 2,
+        out_specs=[pl.BlockSpec(memory_space=pl.ANY)] * len(shapes),
         scratch_shapes=[
             pltpu.SemaphoreType.DMA,
-            pltpu.SemaphoreType.DMA((half,)),
-            pltpu.SemaphoreType.DMA((half,)),
-            pltpu.SemaphoreType.DMA((half, ops)),
-            pltpu.SemaphoreType.DMA((half, ops)),
+            pltpu.SemaphoreType.DMA((colours,)),
+            pltpu.SemaphoreType.DMA((colours,)),
+            pltpu.SemaphoreType.DMA((streams, colours, half)),
+            pltpu.SemaphoreType.DMA((streams, colours, half)),
+            pltpu.SemaphoreType.DMA((streams, colours, half, ops)),
+            pltpu.SemaphoreType.DMA((streams, colours, half, ops)),
         ],
-        compiler_params=pltpu.CompilerParams(collective_id=collective_id, has_side_effects=True),
-        name=f"spread_{collective_id}",
-    )(x)
+        compiler_params=pltpu.CompilerParams(
+            collective_id=1 if first else 2, has_side_effects=True
+        ),
+        cost_estimate=pl.CostEstimate(flops=0, bytes_accessed=16 * size, transcendentals=0),
+        name="spread_first" if first else "spread_second",
+    )(x, y)
 
 
 def apply_kernel(
-    channels, rows, roots, site_charges,
+    channels, rows, roots, site_charges, load,
     order_ref, shift_ref, site_ref, psi_ref, left_ref, right_ref, out_ref, mixed
 ):
     @pl.loop(0, NQ)
@@ -109,7 +178,7 @@
             for q in range(DP):
                 h = lax.rem(2 * NQ - site_charges[q] - g, NQ)
                 terms.append(
-                    jnp.dot(left_ref[h], psi_ref[q * NB + r], preferred_element_type=jnp.float32)
+                    jnp.dot(left_ref[h], load(psi_ref, q * NB + r), preferred_element_type=jnp.float32)
                 )
             for c in range(channels):
                 for p in range(DP):
@@ -135,13 +204,13 @@
             out_ref[order_ref[g * NPB + m]] = total[:, m * B:(m + 1) * B]
 
 
-def apply_all(order, shift, site, psi, left, right, rows, roots):
+def apply_all(order, shift, site, psi, left, right, rows, roots, load):
     channels = right.shape[0]
     height = DP * roots * rows
     smem = pl.BlockSpec(memory_space=pltpu.SMEM)
     vmem = pl.BlockSpec(memory_space=pltpu.VMEM)
     return pl.pallas_call(
-        functools.partial(apply_kernel, channels, rows, roots, site_charge_table),
+        functools.partial(apply_kernel, channels, rows, roots, site_charge_table, load),
         out_shape=jax.ShapeDtypeStruct((NB, height, B), jnp.float32),
         in_specs=[smem, smem, smem, vmem, vmem, vmem],
         out_specs=vmem,
@@ -174,7 +243,6 @@
     right_order = jnp.argsort(right_charge, stable=True).astype(jnp.int32)
     shift = (own_charge[:, 0] + own_charge[:, 1]) % NQ
     site = site_masks(site_operators, own_charge).reshape(-1)
-    partner = [(b, (b + half) % bonds) for b in range(bonds)]
 
     right = right_tiles[:, right_order].transpose(0, 1, 3, 2, 4).reshape(
         channels, NB, chunk, NPB * B
@@ -198,18 +266,30 @@
 
     share = sector_rows // ops
     psi = lax.dynamic_slice_in_dim(wavefunction, op * share, share, 1).astype(jnp.bfloat16)
-    psi = psi.reshape(2, some, share, groups, width).transpose(0, 3, 2, 1, 4)
-    psi = psi.reshape(2, groups, share, some * width)
+    psi = psi.reshape(2, some, share, groups, width).transpose(0, 1, 3, 2, 4)
     kept = lax.dynamic_index_in_dim(psi, part, 0, keepdims=False)
-    came = lax.ppermute(lax.dynamic_index_in_dim(psi, 1 - part, 0, keepdims=False), "bond", partner)
-    piece = jnp.stack([jnp.where(part == 0, kept, came), jnp.where(part == 0, came, kept)])
-    gathered = spread(piece, half, ops, 1)
-    if width == B:
-        psi = gathered.transpose(2, 0, 3, 1, 4, 5).reshape(DP * NB, sector_rows, some * B)
-    else:
-        psi = gathered.reshape(half, ops, 2, share, some, strip).transpose(2, 0, 5, 1, 3, 4)
+    other = lax.dynamic_index_in_dim(psi, 1 - part, 0, keepdims=False)
+    (psi,) = spread(kept, other, half, ops, True)
+
+    def load_whole(ref, block):
+        return ref[block]
+
+    def load_first(ref, block):
+        owner = block // groups
+        t, j, at = owner // half, lax.rem(owner, half), lax.rem(block, groups)
+        return jnp.concatenate(
+            [jnp.concatenate([ref[j, o, t, k, at] for o in range(ops)], 0) for k in range(some)], 1
+        )
+
+    load = load_first
+    if width < B:
+        psi = psi.reshape(half, ops, 2, some, share, strip).transpose(2, 0, 5, 1, 4, 3)
         psi = psi.reshape(DP * NB, B, sector_rows, some).transpose(0, 2, 3, 1)
         psi = psi.reshape(DP * NB, sector_rows, some * B)
+        load = load_whole
+    elif share % 16:
+        psi = psi.transpose(2, 0, 4, 1, 5, 3, 6).reshape(DP * NB, sector_rows, some * B)
+        load = load_whole
 
     def unpack(result):
         result = result.reshape(NB, DP, some, held, B)[:, :, :, :rows]
@@ -224,7 +304,7 @@
             total += lax.ppermute(sent, "op", [(o, (o + e) % ops) for o in range(ops)])
         return total
 
-    first = unpack(apply_all(right_order, shift, site, psi, left, right, held, some))
+    first = unpack(apply_all(right_order, shift, site, psi, left, right, held, some, load))
     turned = (DP * NB, some, NPB, band, B)
     if DP % ops == 0:
         first = summed_share(first, 1).transpose(1, 0, 2, 3, 4, 5)
@@ -235,15 +315,27 @@
 
     mine = lax.dynamic_index_in_dim(first, part, 2, keepdims=False)
     theirs = lax.dynamic_index_in_dim(first, 1 - part, 2, keepdims=False)
-    back = lax.ppermute(theirs.astype(jnp.bfloat16), "bond", partner).astype(jnp.float32)
+    again = first.astype(jnp.bfloat16).transpose(1, 0, 2, 3, 4)
+    again, back = spread(again, theirs.astype(jnp.bfloat16), half, ops, False)
+    back = back.astype(jnp.float32)
     both = jnp.stack([jnp.where(part == 0, mine, back), jnp.where(part == 0, back, mine)])
     sigma_one = both.transpose(0, 2, 3, 1, 4).reshape(roots, band, blocks * B)
 
-    again = first.astype(jnp.bfloat16).transpose(0, 2, 3, 1, 4)
-    again = again.reshape(blocks, NPB, band, some * B)
-    again = spread(again, half, ops, 2)
-    again = again.transpose(1, 2, 3, 0, 4, 5).reshape(DP * NB, sector_rows, some * B)
-    second = unpack(apply_all(right_order, shift, site, again, left, right, held, some))
+    def load_second(ref, block):
+        o, at = block // blocks, lax.rem(block, blocks)
+        return jnp.concatenate(
+            [
+                jnp.concatenate([ref[j, o, 0, k, at, m] for m in range(NPB) for j in range(half)], 0)
+                for k in range(some)
+            ], 1,
+        )
+
+    load = load_second
+    if band % 16:
+        again = again[:, :, 0].transpose(1, 3, 4, 0, 5, 2, 6)
+        again = again.reshape(DP * NB, sector_rows, some * B)
+        load = load_whole
+    second = unpack(apply_all(right_order, shift, site, again, left, right, held, some, load))
     if ops == NPB:
         second = summed_share(second, 3)
     else:

time: 512 us -> 354 us (0.69)
  Pallas kernels: 310 us -> 193 us
  local copies, waits for them, and re-layouts: 52 us -> 30.8 us
  starting transfers between devices: 28.3 us -> 12.5 us
    pallas_call x2, Pallas kernels: 261 us -> 144 us  [spread(): pl.pallas_call(functools.partial(spread_kernel, half, ops, colours, first...]
    ppermute x2 -> x0, waiting for transfers between devices: 85.1 us -> none  [the longest x1 45.2 us: local(): lax.ppermute(lax.dynamic_index_in_dim(psi, 1 - part, 0, keepdims=False),...]
    all_gather x1, waiting for transfers between devices: 0.01 us -> 66.9 us  [local(): lax.all_gather(right, 'bond', axis=2, tiled=True)]
    transpose x4 -> x1, local copies, waits for them, and re-layouts: 24.1 us -> 1.01 us  [local(): again = first.astype(jnp.bfloat16).transpose(1, 0, 2, 3, 4)]
    all_to_all x1, waiting for transfers between devices: 0.01 us -> 18 us  [local(): lax.all_to_all(second, 'bond', split_axis=0, concat_axis=0, tiled=True)]
    all_to_all x1, starting transfers between devices: 15.8 us -> 5.59 us  [local(): lax.all_to_all(second, 'bond', split_axis=0, concat_axis=0, tiled=True)]
  transfers between devices with their start and end apart: 8 -> 6, of which waited for: 4 -> 4; matrix products, arithmetic and copies ran while one was open for 6% -> 5% of each run, Pallas kernels for 26% -> 25%
where the time goes in v2:
time: 354 us
  Pallas kernels  193 us (55%)
  waiting for transfers between devices  91.6 us (26%)
  local copies, waits for them, and re-layouts  30.8 us (9%)
  between operations  14.3 us (4%)
  starting transfers between devices  12.5 us (4%)
  other arithmetic  11 us (3%)
    pallas_call x2, Pallas kernels, spread(): pl.pallas_call(functools.partial(spread_kernel, half, ops, colours, first...  144 us
    all_gather x1, waiting for transfers between devices, local(): lax.all_gather(right, 'bond', axis=2, tiled=True)  66.9 us
    pallas_call x2, Pallas kernels, apply_all(): pl.pallas_call(functools.partial(apply_kernel, channels, rows, roots, sit...  49.6 us
    all_to_all x1, waiting for transfers between devices, local(): lax.all_to_all(second, 'bond', split_axis=0, concat_axis=0, tiled=True)  18 us
  transfers between devices with their start and end apart: 6, of which 4 were waited for; matrix products, arithmetic and copies ran while one was open for 5% of the time, Pallas kernels for 25%

profile of v2, /device:TPU:0, one launch (start us, length us, event | category | flops | bytes accessed | tf_op | source)
XLA Modules:
  0.0 353.6 jit_solution(10204228203852498713)
XLA Ops:
  7.2 0.0 copy-start
  7.2 0.0 copy-start.7
  7.2 0.0 copy-start.8
  7.2 0.0 all-gather.2.cloned.1.call-start
  7.3 2.0 sort.31
  9.3 2.5 gather_fusion.2
  11.8 1.9 copy_bitcast_fusion.1
  13.7 0.0 all-gather.2.cloned.1.call-update
  13.7 5.4 %collective-permute-start = (bf16[8,16,2,8,128]{4,3,2,1,0:T(8,128)(2,1)}, bf16[8,16,2,8,128]{4,3,2,1,0:T(8,128)(2,1)}, u32[]{:S(2)}, u32[]{:S(2)}) collective-permute-start(bf16[8,16,2,8,128]{4,3,2,1,0:T(8,128)(2,1)} %param.9), channel_id=1, source_target_pairs={{0,0},{2,16},{4,2},{6,18},{8,4},{10,20},{12,6},{14,22},{16,8},{18,... | collective-permute-start | bytes 1572872 | tf_op jit(solution)/shard_map/ppermute | solution.py:256
  19.1 1.1 collective-permute-start.1
  20.2 0.1 constant_dynamic-slice_fusion.7
  20.3 0.1 broadcast_add_fusion
  20.4 0.1 fusion.10
  20.5 0.1 copy.41
  20.6 0.6 reshape.129.site_ref
  21.2 1.0 constant_dynamic-slice_fusion.6
  22.2 1.5 copy.55
  23.7 0.0 copy-start.9
  23.7 0.1 constant_dynamic-slice_fusion.4
  23.8 0.9 copy.56
  24.7 0.9 copy.57
  25.7 0.1 compare_select_fusion.1
  25.8 0.1 reshape.141
  25.9 1.3 sort.32
  27.2 1.2 gather_fusion
  28.4 0.1 gather.12
  28.6 0.1 reshape.147
  28.7 88.2 %spread_first.1.psi_ref = bf16[8,2,2,3,4,128,128]{6,5,4,3,2,1,0:T(8,128)(2,1)} custom-call(bf16[3,4,128,128]{3,2,1,0:T(8,128)(2,1)} %bitcast.76, bf16[3,4,128,128]{3,2,1,0:T(8,128)(2,1)} %bitcast.77), custom_call_target="tpu_custom_call" | custom-call | bytes 201326592 | tf_op jit(solution)/shard_map/spread_first/pallas_call | solution.py:147
  117.0 0.6 and_select_fusion.shift_ref
  117.6 0.0 collective-permute-done
  117.6 0.0 collective-permute-done.1
  117.6 1.3 broadcast_select_fusion.1
  118.9 0.2 pad_maximum_fusion
  119.1 0.9 gather_fusion.1
  120.0 1.2 copy.70
  121.2 1.5 reshape.131.left_ref
  122.7 66.9 %all-gather.2.cloned.1.call-done = bf16[8,16,128,256]{3,2,1,0:T(8,128)(2,1)} async-done(((bf16[8,16,8,256]{3,2,1,0:T(8,128)(2,1)}), bf16[8,16,128,256]{3,2,1,0:T(8,128)(2,1)}) %all-gather.2.cloned.1.call-update) | async-done | bytes 8388624 | tf_op jit(solution)/shard_map/all_gather | solution.py:250
  189.6 24.8 %apply_all.2 = f32[16,384,128]{2,1,0:T(8,128)} custom-call(s32[16]{0:T(128)} %copy-done.5, s32[8]{0:T(128)} %and_select_fusion.shift_ref, f32[128]{0:T(128)} %reshape.129.site_ref, bf16[8,2,2,3,4,128,128]{6,5,4,3,2,1,0:T(8,128)(2,1)} %spread_first.1.psi_ref, bf16[8,256,256]{2,1,0:T(8,128)(2,1)} %reshape.131.left_ref, bf16[8,8,256,256]{3,2,1,0:T(8,128)(2,1)} %bitcast.65), custom_call_target="tpu_custom_call" | custom-call | tf_op jit(solution)/shard_map/apply_all/pallas_call | solution.py:212
  214.5 2.4 constant_dynamic-slice_fusion.3
  216.9 1.3 copy.59
  218.2 0.0 collective-permute-start.2
  218.2 3.6 %collective-permute-done.2 = f32[16,2,3,2,16,128]{5,4,2,0,1,3:T(8,128)S(1)} collective-permute-done((f32[16,2,3,2,16,128]{5,4,2,0,1,3:T(8,128)}, f32[16,2,3,2,16,128]{5,4,2,0,1,3:T(8,128)S(1)}, u32[]{:S(2)}, u32[]{:S(2)}) %collective-permute-start.2) | collective-permute-done | bytes 1572896 | tf_op jit(solution)/shard_map/ppermute | solution.py:304
  221.8 1.1 copy-done.2
  223.0 1.6 copy_add_fusion.1
  224.6 0.1 convert_bitcast_fusion.1
  224.7 0.8 fusion.4.refs_1_
  225.5 1.0 copy.49.refs_0_
  226.5 55.4 %spread_second.1 = (bf16[8,2,1,3,32,2,16,128]{7,6,5,4,3,2,1,0:T(8,128)(2,1)}, bf16[32,3,16,128]{3,2,1,0:T(8,128)(2,1)}) custom-call(bf16[3,32,2,16,128]{4,3,2,1,0:T(8,128)(2,1)} %copy.49.refs_0_, bf16[32,3,16,128]{3,2,1,0:T(8,128)(2,1)} %fusion.4.refs_1_), custom_call_target="tpu_custom_call" | custom-call | bytes 201326592 | tf_op jit(solution)/shard_map/spread_second/pallas_call | solution.py:147
  282.0 24.8 %apply_all.3 = f32[16,384,128]{2,1,0:T(8,128)} custom-call(s32[16]{0:T(128)} %copy-done.5, s32[8]{0:T(128)} %and_select_fusion.shift_ref, f32[128]{0:T(128)} %reshape.129.site_ref, bf16[8,2,1,3,32,2,16,128]{7,6,5,4,3,2,1,0:T(8,128)(2,1)} %get-tuple-element.9.psi_ref, bf16[8,256,256]{2,1,0:T(8,128)(2,1)} %reshape.131.left_ref, bf16[8,8,256,256]{3,2,1,0:T(8,128)(2,1)} %bitcast.66), custom_call_target="tpu_custom_call" | custom-call | tf_op jit(solution)/shard_map/apply_all/pallas_call | solution.py:212
  306.8 2.3 constant_dynamic-slice_fusion.1
  309.0 0.9 copy.61
  310.0 0.4 collective-permute-start.3
  310.4 3.0 collective-permute-done.3
  313.4 1.9 fusion.3
  315.3 1.6 reshape.136
  316.9 1.3 copy.53
  318.2 5.6 %all-to-all-start = ((bf16[16,3,16,512]{3,2,1,0:T(8,128)(2,1)}), bf16[16,3,16,512]{3,2,1,0:T(8,128)(2,1)}, u32[]{:S(2)}, u32[]{:S(2)}) async-start(bf16[16,3,16,512]{3,2,1,0:T(8,128)(2,1)} %copy.53), calls=%async_computation | async-start | bytes 1572864 | tf_op jit(solution)/shard_map/all_to_all | solution.py:346
  323.8 0.1 fusion.1
  323.9 0.1 maximum_bitcast_fusion
  324.1 0.5 copy.50
  324.6 1.4 reshape.135
  326.0 18.0 %all-to-all-done = bf16[16,3,16,512]{3,2,1,0:T(8,128)(2,1)} async-done(((bf16[16,3,16,512]{3,2,1,0:T(8,128)(2,1)}), bf16[16,3,16,512]{3,2,1,0:T(8,128)(2,1)}, u32[]{:S(2)}, u32[]{:S(2)}) %all-to-all-start) | async-done | bytes 786464 | tf_op jit(solution)/shard_map/all_to_all | solution.py:346
  344.0 1.5 convert_bitcast_fusion
  345.5 1.3 copy.54
  (23 shorter events, 0.1 us)
Async XLA Ops:
  7.2 14.1 %copy-start = (f32[6,256,512]{2,1,0:T(8,128)S(1)}, f32[6,256,512]{2,1,0:T(8,128)}, u32[]{:S(2)}) copy-start(f32[6,256,512]{2,1,0:T(8,128)} %param.8) | copy-start | bytes 9437188
  7.2 13.1 %copy-start.7 = (s32[4]{0:T(128)S(1)}, s32[4]{0:T(128)}, u32[]{:S(2)}) copy-start(s32[4]{0:T(128)} %constant.104) | copy-start | bytes 52
  7.2 13.1 %copy-start.8 = (s32[4]{0:T(128)S(1)}, s32[4]{0:T(128)}, u32[]{:S(2)}) copy-start(s32[4]{0:T(128)} %constant.101.clone) | copy-start | bytes 52
  7.2 13.0 %copy-start.6 = (s32[16,2]{0,1:T(2,128)S(1)}, s32[16,2]{0,1:T(2,128)}, u32[]{:S(2)}) copy-start(s32[16,2]{0,1:T(2,128)} %param.14) | copy-start | bytes 388
  7.2 13.2 %copy-start.4 = (f32[8,4,4]{0,2,1:T(4,128)S(1)}, f32[8,4,4]{0,2,1:T(4,128)}, u32[]{:S(2)}) copy-start(f32[8,4,4]{0,2,1:T(4,128)} %param.11) | copy-start | bytes 1540
  7.2 182.4 %all-gather.2.cloned.1.call-start = ((), (), s32[]{:S(2)}) async-start(), calls=%async_computation.1 | async-start | bytes 8912896 | tf_op jit(solution)/shard_map/all_gather | solution.py:250
  9.3 12.9 %copy-start.5 = (s32[16]{0:T(128)}, s32[16]{0:T(128)S(1)}, u32[]{:S(2)}) copy-start(s32[16]{0:T(128)S(1)} %get-tuple-element.6.order_ref) | copy-start | bytes 196
  13.7 103.8 %collective-permute-start = (bf16[8,16,2,8,128]{4,3,2,1,0:T(8,128)(2,1)}, bf16[8,16,2,8,128]{4,3,2,1,0:T(8,128)(2,1)}, u32[]{:S(2)}, u32[]{:S(2)}) collective-permute-start(bf16[8,16,2,8,128]{4,3,2,1,0:T(8,128)(2,1)} %param.9), channel_id=1, source_target_pairs={{0,0},{2,16},{4,2},{6,18},{8,4},{10,20},{12,6},{14,22},{16,8},{18,... | collective-permute-start | bytes 1572872 | tf_op jit(solution)/shard_map/ppermute | solution.py:256
  19.1 98.5 %collective-permute-start.1 = (bf16[8,16,2,8,128]{4,3,2,1,0:T(8,128)(2,1)}, bf16[8,16,2,8,128]{4,3,2,1,0:T(8,128)(2,1)}, u32[]{:S(2)}, u32[]{:S(2)}) collective-permute-start(bf16[8,16,2,8,128]{4,3,2,1,0:T(8,128)(2,1)} %param.9), channel_id=1, source_target_pairs={{0,16},{2,0},{4,18},{6,2},{8,20},{10,4},{12,22},{14,6},{16,24},{18... | collective-permute-start | bytes 1572872 | tf_op jit(solution)/shard_map/ppermute | solution.py:257
  23.7 2.2 copy-start.9
  218.2 3.6 %collective-permute-start.2 = (f32[16,2,3,2,16,128]{5,4,2,0,1,3:T(8,128)}, f32[16,2,3,2,16,128]{5,4,2,0,1,3:T(8,128)S(1)}, u32[]{:S(2)}, u32[]{:S(2)}) collective-permute-start(f32[16,2,3,2,16,128]{5,4,2,0,1,3:T(8,128)} %copy.59), channel_id=1, source_target_pairs={{0,1},{1,0},{2,3},{3,2},{4,5},{5,4},{6,7},{7,6},{8,9},{9,8},{10,11... | collective-permute-start | bytes 4718600 | tf_op jit(solution)/shard_map/ppermute | solution.py:304
  221.8 1.1 copy-start.2
  310.0 3.5 collective-permute-start.3
  316.9 6.9 %copy-start.3 = (bf16[32,3,16,128]{3,2,1,0:T(8,128)(2,1)S(1)}, bf16[32,3,16,128]{3,2,1,0:T(8,128)(2,1)}, u32[]{:S(2)}) copy-start(bf16[32,3,16,128]{3,2,1,0:T(8,128)(2,1)} %get-tuple-element.8) | copy-start | bytes 1179652
  318.2 25.8 %all-to-all-start = ((bf16[16,3,16,512]{3,2,1,0:T(8,128)(2,1)}), bf16[16,3,16,512]{3,2,1,0:T(8,128)(2,1)}, u32[]{:S(2)}, u32[]{:S(2)}) async-start(bf16[16,3,16,512]{3,2,1,0:T(8,128)(2,1)} %copy.53), calls=%async_computation | async-start | bytes 1572864 | tf_op jit(solution)/shard_map/all_to_all | solution.py:346
  344.0 2.8 copy-start.1
Sparse Core Ops, SparseCore 0:
  13.8 175.7 all-gather.1
